TPU v7x, 128 devices: a whole 4x4x4 slice. The times are simulated.
128 devices in a mesh: row: 4 (over x), col: 32 (over y, z, core).
Axes of the slice: x: 4, y: 4, z: 4, core: 2. Of those that a mesh axis runs over, the one named last changes fastest.
Arguments:
- node_states: bfloat16 [12288, 512], P(('row', 'col')), may hold values from -6 to 6
- walk_nodes: int32 [1024, 64], P(('row', 'col')), may hold values from 0 to 12287, as said below
- walk_lengths: int32 [1024], P(('row', 'col')), may hold values from 16 to 64
- adjacency: int32 [12288, 12288], P('col', 'row'), may hold values 0 or 1
- w_xz: bfloat16 [2, 512, 2048], replicated, may hold values from -0.25 to 0.25
- w_bc: bfloat16 [2, 512, 256], replicated, may hold values from -0.25 to 0.25
- w_dt: bfloat16 [2, 512, 16], replicated, may hold values from -0.25 to 0.25
- decay_rate: float32 [2, 16], replicated, may hold values from 0.01 to 1
- w_out: bfloat16 [2, 1024, 512], replicated, may hold values from -0.1875 to 0.1875
- w_up: bfloat16 [512, 1024], replicated, may hold values from -0.25 to 0.25
- w_down: bfloat16 [1024, 512], replicated, may hold values from -0.1875 to 0.1875
Outputs:
- refreshed: bfloat16 [12288, 512], P('col')
Inputs may be any that keep to these rules, and one draw needn't show every extreme that they name: `walk_nodes`: among the 8 walks of one device (aligned blocks of walks), at most 8 positions, live or not, fall on the 96 nodes held by any one device (nodes n with the same n // 96).
All inputs are finite; a program needn't handle non-finite values. No bound on the sum of `adjacency` on one device may be relied on, other than what follows from the above.
Results may differ from a plain program's by a relative error of at most 0.018.
Values may be sent and summed in bfloat16 or wider, within the bound.
No kernel may reach another device: no remote copies, remote signals or barrier semaphores. Data moves between devices by JAX's collectives and lax.ppermute only.
A program may use at most 128 MiB of HBM per device.

v0:
```python
import jax
import jax.numpy as jnp
from jax import lax
from jax.sharding import PartitionSpec as P


def encode_walks(first, live, w_xz, w_bc, w_dt, decay_rate, w_out):
    walk_count, walk_len, width = first.shape
    inner_width = w_out.shape[1]
    heads = w_dt.shape[2]
    state_width = w_bc.shape[2] // 2
    head_width = inner_width // heads
    live_mask = live.astype(jnp.float32)
    position_ids = jnp.arange(walk_len, dtype=jnp.int32)
    forward_tri = position_ids[:, None] >= position_ids[None, :]
    backward_tri = position_ids[:, None] <= position_ids[None, :]
    stream = first.reshape(walk_count * walk_len, width)
    for layer_index in range(w_xz.shape[0]):
        widened = stream.astype(jnp.float32)
        normed = (
            widened * lax.rsqrt(jnp.mean(widened * widened, axis=-1, keepdims=True) + 1e-05)
        ).astype(jnp.bfloat16)
        both = jnp.dot(normed, w_xz[layer_index], preferred_element_type=jnp.float32)
        inner = (
            both[:, :inner_width]
            .astype(jnp.bfloat16)
            .reshape(walk_count, walk_len, heads, head_width)
        )
        gate = both[:, inner_width:]
        proj = jnp.dot(normed, w_bc[layer_index], preferred_element_type=jnp.float32).astype(
            jnp.bfloat16
        )
        proj = proj.reshape(walk_count, walk_len, 2 * state_width)
        b_input = proj[..., :state_width]
        c_output = proj[..., state_width:]
        step_size = jax.nn.softplus(
            jnp.dot(normed, w_dt[layer_index], preferred_element_type=jnp.float32)
        )
        step_size = step_size.reshape(walk_count, walk_len, heads)
        log_decay = -decay_rate[layer_index][None, None, :] * step_size
        running = jnp.transpose(jnp.cumsum(log_decay, axis=1), (0, 2, 1))
        before = running - jnp.transpose(log_decay, (0, 2, 1))
        forward_gap = running[:, :, :, None] - running[:, :, None, :]
        backward_gap = before[:, :, None, :] - before[:, :, :, None]
        decay_mat = jnp.where(forward_tri, jnp.exp(jnp.minimum(forward_gap, 0.0)), 0.0)
        decay_mat = decay_mat + jnp.where(
            backward_tri, jnp.exp(jnp.minimum(backward_gap, 0.0)), 0.0
        )
        scores = jnp.einsum(
            "wtk,wsk->wts", c_output, b_input, preferred_element_type=jnp.float32
        ) * state_width ** (-0.5)
        source = jnp.transpose(step_size * live_mask[:, :, None], (0, 2, 1))
        mix = (scores[:, None, :, :] * decay_mat * source[:, :, None, :]).astype(jnp.bfloat16)
        mixed = jnp.einsum("whts,wshp->wthp", mix, inner, preferred_element_type=jnp.float32)
        mixed = mixed.reshape(walk_count * walk_len, inner_width)
        gated = (mixed * jax.nn.silu(gate)).astype(jnp.bfloat16)
        stream = (
            widened + jnp.dot(gated, w_out[layer_index], preferred_element_type=jnp.float32)
        ).astype(jnp.bfloat16)
    return stream


def finish_nodes(combined, w_up, w_down):
    centred = combined - jnp.mean(combined, axis=-1, keepdims=True)
    normal = centred * lax.rsqrt(jnp.mean(centred * centred, axis=-1, keepdims=True) + 1e-05)
    hidden = jax.nn.gelu(
        jnp.dot(normal.astype(jnp.bfloat16), w_up, preferred_element_type=jnp.float32)
    ).astype(jnp.bfloat16)
    return (normal + jnp.dot(hidden, w_down, preferred_element_type=jnp.float32)).astype(
        jnp.bfloat16
    )


def pick_rows(node_states, requests):
    found = requests >= 0
    chosen = node_states[jnp.maximum(requests, 0)]
    return jnp.where(found[:, :, None], chosen, jnp.zeros((), jnp.bfloat16))


def per_device(
    node_states,
    walk_nodes,
    walk_lengths,
    adjacency,
    w_xz,
    w_bc,
    w_dt,
    decay_rate,
    w_out,
    w_up,
    w_down,
):
    node_count, width = node_states.shape
    walk_count, walk_len = walk_nodes.shape
    devices_all = lax.axis_size(("row", "col"))
    tok_count = walk_count * walk_len
    capacity = max(2, 2 * tok_count // devices_all)
    position_ids = jnp.arange(walk_len, dtype=jnp.int32)
    live = position_ids[None, :] < walk_lengths[:, None]
    flat_nodes = walk_nodes.reshape(tok_count)
    flat_live = live.reshape(tok_count)
    owner_ids = flat_nodes // node_count
    local_ids = flat_nodes - owner_ids * node_count
    token_ids = jnp.arange(tok_count, dtype=jnp.int32)
    ordering = jnp.argsort(owner_ids * tok_count + token_ids)
    owner_sorted = owner_ids[ordering]
    owner_range = jnp.arange(devices_all, dtype=jnp.int32)
    per_owner = jnp.sum((owner_ids[:, None] == owner_range[None, :]).astype(jnp.int32), axis=0)
    starts = jnp.cumsum(per_owner) - per_owner
    rank_sorted = token_ids - starts[owner_sorted]
    slot_ids = (
        jnp.zeros((tok_count,), jnp.int32).at[ordering].set(owner_sorted * capacity + rank_sorted)
    )
    wanted = (
        jnp.full((devices_all * capacity,), -1, jnp.int32)
        .at[slot_ids]
        .set(jnp.where(flat_live, local_ids, -1))
    )
    requests = lax.all_to_all(
        wanted.reshape(devices_all, capacity),
        ("row", "col"),
        split_axis=0,
        concat_axis=0,
        tiled=True,
    )
    picked = pick_rows(node_states, requests)
    arrived = lax.all_to_all(picked, ("row", "col"), split_axis=0, concat_axis=0, tiled=True)
    first = arrived.reshape(devices_all * capacity, width)[slot_ids]
    encoded = encode_walks(
        first.reshape(walk_count, walk_len, width), live, w_xz, w_bc, w_dt, decay_rate, w_out
    )
    kept = jnp.where(flat_live[:, None], encoded, jnp.zeros((), jnp.bfloat16))
    outgoing = jnp.zeros((devices_all * capacity, width), jnp.bfloat16).at[slot_ids].set(kept)
    returned = lax.all_to_all(
        outgoing.reshape(devices_all, capacity, width),
        ("row", "col"),
        split_axis=0,
        concat_axis=0,
        tiled=True,
    )
    returned = returned.reshape(devices_all * capacity, width)
    flat_requests = requests.reshape(devices_all * capacity)
    member = flat_requests[None, :] == jnp.arange(node_count, dtype=jnp.int32)[:, None]
    visit_sum = jnp.dot(member.astype(jnp.bfloat16), returned, preferred_element_type=jnp.float32)
    visit_count = jnp.sum(member.astype(jnp.float32), axis=1)
    update = (node_states.astype(jnp.float32) + visit_sum / (1.0 + visit_count)[:, None]).astype(
        jnp.bfloat16
    )
    row_block = adjacency.shape[0]
    row_begin = lax.axis_index("col") * row_block
    col_begin = lax.axis_index("row") * adjacency.shape[1]
    row_global = row_begin + jnp.arange(row_block, dtype=jnp.int32)
    piece = lax.all_gather(update, "col", axis=0, tiled=True)
    piece_rows = piece.shape[0]
    col_global = col_begin + jnp.arange(piece_rows, dtype=jnp.int32)
    self_link = (row_global[:, None] == col_global[None, :]).astype(jnp.int32)
    links = (adjacency + self_link).astype(jnp.bfloat16)
    neighbour_sum = jnp.dot(links, piece, preferred_element_type=jnp.float32)
    combined = lax.psum(neighbour_sum.astype(jnp.bfloat16), "row").astype(jnp.float32)
    return finish_nodes(combined, w_up, w_down)


def solution(mesh):
    return jax.shard_map(
        per_device,
        mesh=mesh,
        in_specs=(
            P(("row", "col"), None),
            P(("row", "col"), None),
            P(("row", "col")),
            P("col", "row"),
            P(),
            P(),
            P(),
            P(),
            P(),
            P(),
            P(),
        ),
        out_specs=P("col", None),
        check_vma=False,
    )
```

profile of v0, /device:TPU:0, one launch (start us, length us, event | category | flops | bytes accessed | tf_op | source)
XLA Modules:
  0.0 278.1 jit_solution(1807728623535561800)
XLA Ops:
  8.4 3.8 %sort.17 = (s32[512]{0:T(512)}, s32[512]{0:T(512)S(1)}) sort(s32[512]{0:T(512)S(1)} %iota_add_fusion.1, s32[512]{0:T(512)S(1)} %iota.44), dimensions={0}, to_apply=%region_0.1 | sort | flops 4608 | bytes 8192 | tf_op jit(solution)/shard_map/jit(argsort)/sort | solution.py:105
  12.2 3.5 %gather_fusion = s32[512]{0:T(512)S(1)} fusion(s32[512]{0:T(512)S(1)} %get-tuple-element.8, s32[1024]{0:T(1024)S(1)} %pad_clamp_fusion.2), kind=kCustom, calls=%fused_computation | custom fusion | bytes 6144 | tf_op jit(solution)/shard_map/gather | solution.py:106
  16.1 3.3 %gather_fusion.1 = s32[512]{0:T(512)S(1)} fusion(s32[128]{0:T(128)S(1)} %sub.82, s32[1024]{0:T(1024)S(1)} %pad_clamp_fusion.1), kind=kCustom, calls=%fused_computation.1 | custom fusion | bytes 6144 | tf_op jit(solution)/shard_map/gather | solution.py:110
  19.5 2.4 scatter_custom_fusion
  21.9 2.4 scatter_custom_fusion.1
  24.5 20.5 %all_to_all.19 = s32[128,1,8]{2,1,0:T(1,128)S(1)} all-to-all(s32[128,1,8]{2,1,0:T(1,128)S(1)} %bitcast.84), channel_id=1, replica_groups=mesh['row'=4,'col'=32] {'row','col'}, dimensions={0} | all-to-all | bytes 8192 | tf_op jit(solution)/shard_map/all_to_all | solution.py:119
  45.4 4.0 %gather_fusion.2 = bf16[1024,512]{1,0:T(8,128)(2,1)S(1)} fusion(bf16[96,512]{1,0:T(8,128)(2,1)S(1)} %copy-done.1, s32[1024]{0:T(1024)S(1)} %broadcast_clamp_fusion), kind=kCustom, calls=%fused_computation.2 | custom fusion | bytes 2101248 | tf_op jit(solution)/shard_map/gather | solution.py:76
  50.6 4.8 %all-to-all-start.1 = ((bf16[128,8,512]{2,1,0:T(8,128)(2,1)}), bf16[128,8,512]{2,1,0:T(8,128)(2,1)S(1)}, u32[]{:S(2)}, u32[]{:S(2)}) async-start(bf16[128,8,512]{2,1,0:T(8,128)(2,1)} %bitcast_select_fusion), calls=%async_computation.1 | async-start | bytes 2097152 | tf_op jit(solution)/shard_map/all_to_all | solution.py:127
  55.5 19.1 %all-to-all-done.1 = bf16[128,8,512]{2,1,0:T(8,128)(2,1)S(1)} async-done(((bf16[128,8,512]{2,1,0:T(8,128)(2,1)}), bf16[128,8,512]{2,1,0:T(8,128)(2,1)S(1)}, u32[]{:S(2)}, u32[]{:S(2)}) %all-to-all-start.1) | async-done | bytes 1048608 | tf_op jit(solution)/shard_map/all_to_all | solution.py:127
  74.6 2.0 gather_fusion.3
  77.5 6.3 %fusion.112 = f32[8,64,16]{2,0,1:T(8,128)S(1)} fusion(f32[8,64,16]{2,0,1:T(8,128)S(1)} %copy.147), kind=kOutput, calls=%fused_computation.165 | output fusion | flops 516096 | bytes 65536 | tf_op jit(solution)/shard_map/jit(cumsum)/reduce_window_sum | solution.py:41
  85.6 2.9 %fusion.5 = f32[512,2048]{1,0:T(8,128)S(1)} fusion(bf16[2,512,2048]{2,1,0:T(8,128)(2,1)} %param.15, bf16[512,512]{0,1:T(8,128)(2,1)S(1)} %copy.145, f32[512]{0:T(512)S(1)} %add_rsqrt_fusion.2), kind=kOutput, calls=%fused_computation.20 | convolution fusion | flops 1074528256 | bytes 6817792 | tf_op jit(solution)/shard_map/dot_general | solution.py:23
  88.5 1.9 copy-done.2
  90.6 2.3 reshape.227
  92.9 6.4 %convolution_bitcast_fusion.1 = f32[8,64,16,64]{1,3,2,0:T(8,128)} fusion(bf16[8,64,16,64]{3,2,1,0:T(8,128)(2,1)} %reshape.227, f32[8,16,64]{2,1,0:T(8,128)S(1)} %copy.149, f32[8,16,64]{2,1,0:T(8,128)S(1)} %bitcast_subtract_fusion.1, f32[8,16,64]{2,1,0:T(8,128)S(1)} %bitcast.80, f32[8,64,64]{2,1,0:T(8,128)S(1)} %convolution_multiply_fusion.1, ...), kind=kOutput, calls=%fused_computation.15 | convolution fusion | flops 72351744 | bytes 3383296 | tf_op jit(solution)/shard_map/whts,wshp->wthp/dot_general | solution.py:54
  99.3 5.6 %copy.151 = f32[8,64,16,64]{3,2,1,0:T(8,128)} copy(f32[8,64,16,64]{1,3,2,0:T(8,128)} %convolution_bitcast_fusion.1) | data formatting | bytes 4194304 | tf_op jit(solution)/shard_map/whts,wshp->wthp/transpose | solution.py:54
  104.9 4.9 %reshape.230 = f32[512,1024]{1,0:T(8,128)} reshape(f32[8,64,16,64]{3,2,1,0:T(8,128)} %copy.151) | data formatting | bytes 4194304 | tf_op jit(solution)/shard_map/reshape | solution.py:55
  109.8 3.6 %fusion.46 = (f32[512]{0:T(512)S(1)}, bf16[512,512]{0,1:T(8,128)(2,1)S(1)}) fusion(bf16[2,1024,512]{2,1,0:T(8,128)(2,1)} %param.19, f32[512,1024]{1,0:T(8,128)} %reshape.230, f32[512,2048]{1,0:T(8,128)} %copy-done.2, bf16[512,512]{0,1:T(8,128)(2,1)S(1)} %copy.145), kind=kOutput, calls=%fused_computation.75 | convolution fusion | flops 541588992 | bytes 6293504 | tf_op jit(solution)/shard_map/dot_general | solution.py:58
  114.3 3.2 %fusion.3 = f32[512,2048]{1,0:T(8,128)} fusion(bf16[2,512,2048]{2,1,0:T(8,128)(2,1)S(1)} %copy-done.3, bf16[512,512]{0,1:T(8,128)(2,1)S(1)} %get-tuple-element.14, f32[512]{0:T(512)S(1)} %add_rsqrt_fusion.1), kind=kOutput, calls=%fused_computation.18 | convolution fusion | flops 1074528256 | bytes 6817792 | tf_op jit(solution)/shard_map/dot_general | solution.py:23
  117.8 6.3 %fusion.113 = f32[8,64,16]{2,0,1:T(8,128)S(1)} fusion(f32[8,64,16]{2,0,1:T(8,128)S(1)} %copy.153), kind=kOutput, calls=%fused_computation.166 | output fusion | flops 516096 | bytes 65536 | tf_op jit(solution)/shard_map/jit(cumsum)/reduce_window_sum | solution.py:41
  126.3 2.3 reshape.231
  128.7 6.4 %convolution_bitcast_fusion = f32[8,64,16,64]{1,3,2,0:T(8,128)} fusion(bf16[8,64,16,64]{3,2,1,0:T(8,128)(2,1)} %reshape.231, f32[8,16,64]{2,1,0:T(8,128)S(1)} %copy.155, f32[8,16,64]{2,1,0:T(8,128)S(1)} %bitcast_subtract_fusion, f32[8,16,64]{2,1,0:T(8,128)S(1)} %bitcast.81, f32[8,64,64]{2,1,0:T(8,128)S(1)} %convolution_multiply_fusion, ...), kind=kOutput, calls=%fused_computation.14 | convolution fusion | flops 72351744 | bytes 3383296 | tf_op jit(solution)/shard_map/whts,wshp->wthp/dot_general | solution.py:54
  135.1 5.6 %copy.157 = f32[8,64,16,64]{3,2,1,0:T(8,128)} copy(f32[8,64,16,64]{1,3,2,0:T(8,128)} %convolution_bitcast_fusion) | data formatting | bytes 4194304 | tf_op jit(solution)/shard_map/whts,wshp->wthp/transpose | solution.py:54
  140.7 3.5 %reshape.234 = f32[512,1024]{1,0:T(8,128)S(1)} reshape(f32[8,64,16,64]{3,2,1,0:T(8,128)} %copy.157) | data formatting | bytes 4194304 | tf_op jit(solution)/shard_map/reshape | solution.py:55
  144.2 3.8 %fusion.41 = bf16[512,512]{0,1:T(8,128)(2,1)} fusion(bf16[512,512]{0,1:T(8,128)(2,1)} %copy-done.4, bf16[2,1024,512]{2,1,0:T(8,128)(2,1)} %param.19, f32[512,1024]{1,0:T(8,128)S(1)} %reshape.234, f32[512,2048]{1,0:T(8,128)} %fusion.3, pred[512]{0:T(512)(128)(4,1)S(1)} %lt.51), kind=kOutput, calls=%fused_computation.65 | convolution fusion | flops 541065216 | bytes 6291968 | tf_op jit(solution)/shard_map/dot_general | solution.py:58
  149.2 3.5 %scatter_custom_fusion.2 = bf16[1024,512]{1,0:T(8,128)(2,1)} fusion(s32[512]{0:T(512)S(1)} %compare_select_fusion.3, bf16[512,512]{1,0:T(8,128)(2,1)S(1)} %copy.159, bf16[]{:T(256)} %constant.37.clone.1), kind=kCustom, calls=%fused_computation.92 | custom fusion | bytes 1048578 | tf_op jit(solution)/shard_map/scatter | solution.py:133
  152.7 4.6 %all-to-all-start.2 = ((bf16[128,8,512]{2,1,0:T(8,128)(2,1)}), bf16[128,8,512]{2,1,0:T(8,128)(2,1)S(1)}, u32[]{:S(2)}, u32[]{:S(2)}) async-start(bf16[128,8,512]{2,1,0:T(8,128)(2,1)} %bitcast.27), calls=%async_computation.2 | async-start | bytes 2097152 | tf_op jit(solution)/shard_map/all_to_all | solution.py:134
  159.0 17.7 %all-to-all-done.2 = bf16[128,8,512]{2,1,0:T(8,128)(2,1)S(1)} async-done(((bf16[128,8,512]{2,1,0:T(8,128)(2,1)}), bf16[128,8,512]{2,1,0:T(8,128)(2,1)S(1)}, u32[]{:S(2)}, u32[]{:S(2)}) %all-to-all-start.2) | async-done | bytes 1048608 | tf_op jit(solution)/shard_map/all_to_all | solution.py:134
  177.8 40.7 %all-gather.2.cloned.1.call-done = bf16[3072,512]{1,0:T(8,128)(2,1)} async-done(((bf16[96,512]{1,0:T(8,128)(2,1)}), bf16[3072,512]{1,0:T(8,128)(2,1)}) %all-gather.2.cloned.1.call-update) | async-done | bytes 3145744 | tf_op jit(solution)/shard_map/all_gather | solution.py:153
  218.5 5.5 %fusion.40 = bf16[384,512]{1,0:T(8,128)(2,1)} fusion(bf16[3072,512]{1,0:T(8,128)(2,1)} %all-gather.2.cloned.1.call-done, s32[384,3072]{1,0:T(8,128)} %param.14, s32[3072]{0:T(1024)S(1)} %iota_add_fusion, s32[384]{0:T(512)S(1)} %iota_add_fusion.2), kind=kOutput, calls=%fused_computation.64 | convolution fusion | flops 1212874752 | bytes 8271360 | tf_op jit(solution)/shard_map/dot_general | solution.py:158
  224.0 41.7 %all-reduce.2.cloned.1.call-done = bf16[384,512]{1,0:T(8,128)(2,1)} async-done(((bf16[384,512]{1,0:T(8,128)(2,1)}), bf16[384,512]{1,0:T(8,128)(2,1)}) %all-reduce.2.cloned.1.call-update) | async-done | bytes 393232 | tf_op jit(solution)/shard_map/psum | solution.py:159
  268.1 3.1 %fusion.39 = bf16[384,512]{1,0:T(8,128)(2,1)} fusion(bf16[1024,512]{1,0:T(8,128)(2,1)S(1)} %copy-done, bf16[384,512]{1,0:T(8,128)(2,1)} %all-reduce.2.cloned.1.call-done, bf16[512,1024]{1,0:T(8,128)(2,1)S(1)} %copy-done.6, f32[384]{0:T(512)S(1)} %add_rsqrt_fusion, f32[384]{0:T(512)S(1)} %broadcast_multiply_fusion), kind=kOutput, calls=%fused_computation.63 | convolution fusion | flops 810614784 | bytes 2886656 | tf_op jit(solution)/shard_map/dot_general | solution.py:69
  (89 shorter events, 16.3 us)
Async XLA Ops:
  6.5 261.6 %copy-start = (bf16[1024,512]{1,0:T(8,128)(2,1)S(1)}, bf16[1024,512]{1,0:T(8,128)(2,1)}, u32[]{:S(2)}) copy-start(bf16[1024,512]{1,0:T(8,128)(2,1)} %param.21) | copy-start | bytes 3145732
  6.5 38.9 %copy-start.1 = (bf16[96,512]{1,0:T(8,128)(2,1)S(1)}, bf16[96,512]{1,0:T(8,128)(2,1)}, u32[]{:S(2)}) copy-start(bf16[96,512]{1,0:T(8,128)(2,1)} %param.11) | copy-start | bytes 294916
  49.4 6.1 %copy-start.5 = (f32[2,16]{1,0:T(2,128)S(1)}, f32[2,16]{1,0:T(2,128)}, u32[]{:S(2)}) copy-start(f32[2,16]{1,0:T(2,128)} %param.18) | copy-start | bytes 388
  50.6 24.0 %all-to-all-start.1 = ((bf16[128,8,512]{2,1,0:T(8,128)(2,1)}), bf16[128,8,512]{2,1,0:T(8,128)(2,1)S(1)}, u32[]{:S(2)}, u32[]{:S(2)}) async-start(bf16[128,8,512]{2,1,0:T(8,128)(2,1)} %bitcast_select_fusion), calls=%async_computation.1 | async-start | bytes 2097152 | tf_op jit(solution)/shard_map/all_to_all | solution.py:127
  74.6 2.4 copy-start.8
  88.5 1.9 copy-start.2
  109.8 3.9 %copy-start.7 = (bf16[2,512,256]{2,1,0:T(8,128)(2,1)S(1)}, bf16[2,512,256]{2,1,0:T(8,128)(2,1)}, u32[]{:S(2)}) copy-start(bf16[2,512,256]{2,1,0:T(8,128)(2,1)} %param.16) | copy-start | bytes 1572868
  109.8 4.5 %copy-start.3 = (bf16[2,512,2048]{2,1,0:T(8,128)(2,1)S(1)}, bf16[2,512,2048]{2,1,0:T(8,128)(2,1)}, u32[]{:S(2)}) copy-start(bf16[2,512,2048]{2,1,0:T(8,128)(2,1)} %param.15) | copy-start | bytes 12582916
  113.4 0.8 copy-start.4
  152.7 24.0 %all-to-all-start.2 = ((bf16[128,8,512]{2,1,0:T(8,128)(2,1)}), bf16[128,8,512]{2,1,0:T(8,128)(2,1)S(1)}, u32[]{:S(2)}, u32[]{:S(2)}) async-start(bf16[128,8,512]{2,1,0:T(8,128)(2,1)} %bitcast.27), calls=%async_computation.2 | async-start | bytes 2097152 | tf_op jit(solution)/shard_map/all_to_all | solution.py:134
  157.4 61.2 %all-gather.2.cloned.1.call-start = ((), (), s32[]{:S(2)}) async-start(), calls=%async_computation.3 | async-start | bytes 3244032 | tf_op jit(solution)/shard_map/all_gather | solution.py:153
  177.7 88.0 %all-reduce.2.cloned.1.call-start = ((), (), s32[]{:S(2)}) async-start(), calls=%async_computation.4 | async-start | bytes 786432 | tf_op jit(solution)/shard_map/psum | solution.py:159
  177.8 90.4 %copy-start.6 = (bf16[512,1024]{1,0:T(8,128)(2,1)S(1)}, bf16[512,1024]{1,0:T(8,128)(2,1)}, u32[]{:S(2)}) copy-start(bf16[512,1024]{1,0:T(8,128)(2,1)} %param.20) | copy-start | bytes 3145732
Sparse Core Ops, SparseCore 0:
  177.8 40.6 all-gather.1
  224.2 41.5 all-reduce.1
where the time goes:
time: 279 us; the launch traced here: 278 us
  waiting for transfers between devices  119 us (43%)
  local copies, waits for them, and re-layouts  53.7 us (19%)
  matrix products  38.5 us (14%)
  other arithmetic  22.7 us (8%)
  blocking collectives  20.5 us (7%)
  between operations  13.8 us (5%)
  starting transfers between devices  9.52 us (3%)
    psum x1, waiting for transfers between devices, per_device(): lax.psum(neighbour_sum.astype(jnp.bfloat16), 'row').astype(jnp.float32)  41.7 us
    all_gather x1, waiting for transfers between devices, per_device(): piece = lax.all_gather(update, 'col', axis=0, tiled=True)  40.7 us
    all_to_all x1, blocking collectives, per_device(): lax.all_to_all(wanted.reshape(devices_all, capacity), ('row', 'col'), spl...  20.5 us
    all_to_all x1, waiting for transfers between devices, per_device(): lax.all_to_all(picked, ('row', 'col'), split_axis=0, concat_axis=0, tiled...  19.1 us
    all_to_all x1, waiting for transfers between devices, per_device(): lax.all_to_all(outgoing.reshape(devices_all, capacity, width), ('row', 'c...  17.7 us
    dot_general x2, matrix products, encode_walks(): jnp.einsum('whts,wshp->wthp', mix, inner, preferred_element_type=jnp.floa...  12.9 us
    another operation x2, other arithmetic, encode_walks(): running = jnp.transpose(jnp.cumsum(log_decay, axis=1), (0, 2, 1))  12.7 us
    transpose x2, local copies, waits for them, and re-layouts, encode_walks(): jnp.einsum('whts,wshp->wthp', mix, inner, preferred_element_type=jnp.floa...  11.2 us
  transfers between devices with their start and end apart: 4, of which 4 were waited for; matrix products, arithmetic and copies ran while one was open for 1% of the time, Pallas kernels for 0%

commit v1 on v0

--- a/solution.py
+++ b/solution.py
@@ -2,6 +2,12 @@
 import jax.numpy as jnp
 from jax import lax
 from jax.sharding import PartitionSpec as P
+
+
+def gather_and_add(x, axis):
+    shards = lax.all_gather(x, axis, axis=0, tiled=False)
+    total = shards.sum(axis=0)
+    return total
 
 
 def encode_walks(first, live, w_xz, w_bc, w_dt, decay_rate, w_out):
@@ -156,7 +162,7 @@
     self_link = (row_global[:, None] == col_global[None, :]).astype(jnp.int32)
     links = (adjacency + self_link).astype(jnp.bfloat16)
     neighbour_sum = jnp.dot(links, piece, preferred_element_type=jnp.float32)
-    combined = lax.psum(neighbour_sum.astype(jnp.bfloat16), "row").astype(jnp.float32)
+    combined = gather_and_add(neighbour_sum.astype(jnp.bfloat16), "row").astype(jnp.float32)
     return finish_nodes(combined, w_up, w_down)
 
 

time: 279 us -> 262 us (0.939)
  waiting for transfers between devices: 119 us -> 103 us
    psum x1 -> x0, waiting for transfers between devices: 41.7 us -> none  [per_device(): lax.psum(neighbour_sum.astype(jnp.bfloat16), 'row').astype(jnp.float32)]
    all_gather x0 -> x1, waiting for transfers between devices: none -> 25.8 us  [gather_and_add(): shards = lax.all_gather(x, axis, axis=0, tiled=False)]
where the time goes in v1:
time: 262 us; the launch traced here: 261 us
  waiting for transfers between devices  103 us (39%)
  local copies, waits for them, and re-layouts  53.7 us (20%)
  matrix products  37.4 us (14%)
  other arithmetic  22.6 us (9%)
  blocking collectives  20.5 us (8%)
  between operations  13.8 us (5%)
  starting transfers between devices  9.52 us (4%)
    all_gather x1, waiting for transfers between devices, per_device(): piece = lax.all_gather(update, 'col', axis=0, tiled=True)  40.8 us
    all_gather x1, waiting for transfers between devices, gather_and_add(): shards = lax.all_gather(x, axis, axis=0, tiled=False)  25.8 us
    all_to_all x1, blocking collectives, per_device(): lax.all_to_all(wanted.reshape(devices_all, capacity), ('row', 'col'), spl...  20.5 us
    all_to_all x1, waiting for transfers between devices, per_device(): lax.all_to_all(picked, ('row', 'col'), split_axis=0, concat_axis=0, tiled...  19.1 us
    all_to_all x1, waiting for transfers between devices, per_device(): lax.all_to_all(outgoing.reshape(devices_all, capacity, width), ('row', 'c...  17.7 us
    dot_general x2, matrix products, encode_walks(): jnp.einsum('whts,wshp->wthp', mix, inner, preferred_element_type=jnp.floa...  12.9 us
    another operation x2, other arithmetic, encode_walks(): running = jnp.transpose(jnp.cumsum(log_decay, axis=1), (0, 2, 1))  12.7 us
    transpose x2, local copies, waits for them, and re-layouts, encode_walks(): jnp.einsum('whts,wshp->wthp', mix, inner, preferred_element_type=jnp.floa...  11.2 us
  transfers between devices with their start and end apart: 4, of which 4 were waited for; matrix products, arithmetic and copies ran while one was open for 1% of the time, Pallas kernels for 0%

profile of v1, /device:TPU:0, one launch (start us, length us, event | category | flops | bytes accessed | tf_op | source)
XLA Modules:
  0.0 261.0 jit_solution(1381012875512830730)
XLA Ops:
  8.4 3.8 %sort.17 = (s32[512]{0:T(512)}, s32[512]{0:T(512)S(1)}) sort(s32[512]{0:T(512)S(1)} %iota_add_fusion.1, s32[512]{0:T(512)S(1)} %iota.44), dimensions={0}, to_apply=%region_0.1 | sort | flops 4608 | bytes 8192 | tf_op jit(solution)/shard_map/jit(argsort)/sort | solution.py:111
  12.2 3.5 %gather_fusion = s32[512]{0:T(512)S(1)} fusion(s32[512]{0:T(512)S(1)} %get-tuple-element.8, s32[1024]{0:T(1024)S(1)} %pad_clamp_fusion.2), kind=kCustom, calls=%fused_computation | custom fusion | bytes 6144 | tf_op jit(solution)/shard_map/gather | solution.py:112
  16.1 3.3 %gather_fusion.1 = s32[512]{0:T(512)S(1)} fusion(s32[128]{0:T(128)S(1)} %sub.82, s32[1024]{0:T(1024)S(1)} %pad_clamp_fusion.1), kind=kCustom, calls=%fused_computation.1 | custom fusion | bytes 6144 | tf_op jit(solution)/shard_map/gather | solution.py:116
  19.5 2.4 scatter_custom_fusion
  21.9 2.4 scatter_custom_fusion.1
  24.5 20.5 %all_to_all.19 = s32[128,1,8]{2,1,0:T(1,128)S(1)} all-to-all(s32[128,1,8]{2,1,0:T(1,128)S(1)} %bitcast.86), channel_id=1, replica_groups=mesh['row'=4,'col'=32] {'row','col'}, dimensions={0} | all-to-all | bytes 8192 | tf_op jit(solution)/shard_map/all_to_all | solution.py:125
  45.4 4.0 %gather_fusion.2 = bf16[1024,512]{1,0:T(8,128)(2,1)S(1)} fusion(bf16[96,512]{1,0:T(8,128)(2,1)S(1)} %copy-done.1, s32[1024]{0:T(1024)S(1)} %broadcast_clamp_fusion), kind=kCustom, calls=%fused_computation.2 | custom fusion | bytes 2101248 | tf_op jit(solution)/shard_map/gather | solution.py:82
  50.6 4.8 %all-to-all-start.1 = ((bf16[128,8,512]{2,1,0:T(8,128)(2,1)}), bf16[128,8,512]{2,1,0:T(8,128)(2,1)S(1)}, u32[]{:S(2)}, u32[]{:S(2)}) async-start(bf16[128,8,512]{2,1,0:T(8,128)(2,1)} %bitcast_select_fusion), calls=%async_computation.1 | async-start | bytes 2097152 | tf_op jit(solution)/shard_map/all_to_all | solution.py:133
  55.5 19.1 %all-to-all-done.1 = bf16[128,8,512]{2,1,0:T(8,128)(2,1)S(1)} async-done(((bf16[128,8,512]{2,1,0:T(8,128)(2,1)}), bf16[128,8,512]{2,1,0:T(8,128)(2,1)S(1)}, u32[]{:S(2)}, u32[]{:S(2)}) %all-to-all-start.1) | async-done | bytes 1048608 | tf_op jit(solution)/shard_map/all_to_all | solution.py:133
  74.6 2.0 gather_fusion.3
  77.5 6.3 %fusion.112 = f32[8,64,16]{2,0,1:T(8,128)S(1)} fusion(f32[8,64,16]{2,0,1:T(8,128)S(1)} %copy.147), kind=kOutput, calls=%fused_computation.165 | output fusion | flops 516096 | bytes 65536 | tf_op jit(solution)/shard_map/jit(cumsum)/reduce_window_sum | solution.py:47
  85.6 2.9 %fusion.5 = f32[512,2048]{1,0:T(8,128)S(1)} fusion(bf16[2,512,2048]{2,1,0:T(8,128)(2,1)} %param.15, bf16[512,512]{0,1:T(8,128)(2,1)S(1)} %copy.145, f32[512]{0:T(512)S(1)} %add_rsqrt_fusion.2), kind=kOutput, calls=%fused_computation.20 | convolution fusion | flops 1074528256 | bytes 6817792 | tf_op jit(solution)/shard_map/dot_general | solution.py:29
  88.5 1.9 copy-done.2
  90.6 2.3 reshape.227
  92.9 6.4 %convolution_bitcast_fusion.1 = f32[8,64,16,64]{1,3,2,0:T(8,128)} fusion(bf16[8,64,16,64]{3,2,1,0:T(8,128)(2,1)} %reshape.227, f32[8,16,64]{2,1,0:T(8,128)S(1)} %copy.149, f32[8,16,64]{2,1,0:T(8,128)S(1)} %bitcast_subtract_fusion.1, f32[8,16,64]{2,1,0:T(8,128)S(1)} %bitcast.82, f32[8,64,64]{2,1,0:T(8,128)S(1)} %convolution_multiply_fusion.1, ...), kind=kOutput, calls=%fused_computation.15 | convolution fusion | flops 72351744 | bytes 3383296 | tf_op jit(solution)/shard_map/whts,wshp->wthp/dot_general | solution.py:60
  99.3 5.6 %copy.151 = f32[8,64,16,64]{3,2,1,0:T(8,128)} copy(f32[8,64,16,64]{1,3,2,0:T(8,128)} %convolution_bitcast_fusion.1) | data formatting | bytes 4194304 | tf_op jit(solution)/shard_map/whts,wshp->wthp/transpose | solution.py:60
  104.9 4.9 %reshape.230 = f32[512,1024]{1,0:T(8,128)} reshape(f32[8,64,16,64]{3,2,1,0:T(8,128)} %copy.151) | data formatting | bytes 4194304 | tf_op jit(solution)/shard_map/reshape | solution.py:61
  109.8 3.6 %fusion.46 = (f32[512]{0:T(512)S(1)}, bf16[512,512]{0,1:T(8,128)(2,1)S(1)}) fusion(bf16[2,1024,512]{2,1,0:T(8,128)(2,1)} %param.19, f32[512,1024]{1,0:T(8,128)} %reshape.230, f32[512,2048]{1,0:T(8,128)} %copy-done.2, bf16[512,512]{0,1:T(8,128)(2,1)S(1)} %copy.145), kind=kOutput, calls=%fused_computation.75 | convolution fusion | flops 541588992 | bytes 6293504 | tf_op jit(solution)/shard_map/dot_general | solution.py:64
  114.3 3.2 %fusion.3 = f32[512,2048]{1,0:T(8,128)} fusion(bf16[2,512,2048]{2,1,0:T(8,128)(2,1)S(1)} %copy-done.3, bf16[512,512]{0,1:T(8,128)(2,1)S(1)} %get-tuple-element.14, f32[512]{0:T(512)S(1)} %add_rsqrt_fusion.1), kind=kOutput, calls=%fused_computation.18 | convolution fusion | flops 1074528256 | bytes 6817792 | tf_op jit(solution)/shard_map/dot_general | solution.py:29
  117.8 6.3 %fusion.113 = f32[8,64,16]{2,0,1:T(8,128)S(1)} fusion(f32[8,64,16]{2,0,1:T(8,128)S(1)} %copy.153), kind=kOutput, calls=%fused_computation.166 | output fusion | flops 516096 | bytes 65536 | tf_op jit(solution)/shard_map/jit(cumsum)/reduce_window_sum | solution.py:47
  126.3 2.3 reshape.231
  128.7 6.4 %convolution_bitcast_fusion = f32[8,64,16,64]{1,3,2,0:T(8,128)} fusion(bf16[8,64,16,64]{3,2,1,0:T(8,128)(2,1)} %reshape.231, f32[8,16,64]{2,1,0:T(8,128)S(1)} %copy.155, f32[8,16,64]{2,1,0:T(8,128)S(1)} %bitcast_subtract_fusion, f32[8,16,64]{2,1,0:T(8,128)S(1)} %bitcast.83, f32[8,64,64]{2,1,0:T(8,128)S(1)} %convolution_multiply_fusion, ...), kind=kOutput, calls=%fused_computation.14 | convolution fusion | flops 72351744 | bytes 3383296 | tf_op jit(solution)/shard_map/whts,wshp->wthp/dot_general | solution.py:60
  135.1 5.6 %copy.157 = f32[8,64,16,64]{3,2,1,0:T(8,128)} copy(f32[8,64,16,64]{1,3,2,0:T(8,128)} %convolution_bitcast_fusion) | data formatting | bytes 4194304 | tf_op jit(solution)/shard_map/whts,wshp->wthp/transpose | solution.py:60
  140.7 3.5 %reshape.234 = f32[512,1024]{1,0:T(8,128)S(1)} reshape(f32[8,64,16,64]{3,2,1,0:T(8,128)} %copy.157) | data formatting | bytes 4194304 | tf_op jit(solution)/shard_map/reshape | solution.py:61
  144.2 3.8 %fusion.41 = bf16[512,512]{0,1:T(8,128)(2,1)} fusion(bf16[512,512]{0,1:T(8,128)(2,1)} %copy-done.4, bf16[2,1024,512]{2,1,0:T(8,128)(2,1)} %param.19, f32[512,1024]{1,0:T(8,128)S(1)} %reshape.234, f32[512,2048]{1,0:T(8,128)} %fusion.3, pred[512]{0:T(512)(128)(4,1)S(1)} %lt.51), kind=kOutput, calls=%fused_computation.65 | convolution fusion | flops 541065216 | bytes 6291968 | tf_op jit(solution)/shard_map/dot_general | solution.py:64
  149.2 3.5 %scatter_custom_fusion.2 = bf16[1024,512]{1,0:T(8,128)(2,1)} fusion(s32[512]{0:T(512)S(1)} %compare_select_fusion.3, bf16[512,512]{1,0:T(8,128)(2,1)S(1)} %copy.159, bf16[]{:T(256)} %constant.39.clone.1), kind=kCustom, calls=%fused_computation.92 | custom fusion | bytes 1048578 | tf_op jit(solution)/shard_map/scatter | solution.py:139
  152.7 4.6 %all-to-all-start.2 = ((bf16[128,8,512]{2,1,0:T(8,128)(2,1)}), bf16[128,8,512]{2,1,0:T(8,128)(2,1)S(1)}, u32[]{:S(2)}, u32[]{:S(2)}) async-start(bf16[128,8,512]{2,1,0:T(8,128)(2,1)} %bitcast.27), calls=%async_computation.2 | async-start | bytes 2097152 | tf_op jit(solution)/shard_map/all_to_all | solution.py:140
  159.0 17.7 %all-to-all-done.2 = bf16[128,8,512]{2,1,0:T(8,128)(2,1)S(1)} async-done(((bf16[128,8,512]{2,1,0:T(8,128)(2,1)}), bf16[128,8,512]{2,1,0:T(8,128)(2,1)S(1)}, u32[]{:S(2)}, u32[]{:S(2)}) %all-to-all-start.2) | async-done | bytes 1048608 | tf_op jit(solution)/shard_map/all_to_all | solution.py:140
  177.8 40.8 %all-gather.4.cloned.1.call-done = bf16[3072,512]{1,0:T(8,128)(2,1)} async-done(((bf16[96,512]{1,0:T(8,128)(2,1)}), bf16[3072,512]{1,0:T(8,128)(2,1)}) %all-gather.4.cloned.1.call-update) | async-done | bytes 3145744 | tf_op jit(solution)/shard_map/all_gather | solution.py:159
  218.5 5.5 %fusion.40 = bf16[384,512]{1,0:T(8,128)(2,1)} fusion(bf16[3072,512]{1,0:T(8,128)(2,1)} %all-gather.4.cloned.1.call-done, s32[384,3072]{1,0:T(8,128)} %param.14, s32[3072]{0:T(1024)S(1)} %iota_add_fusion, s32[384]{0:T(512)S(1)} %iota_add_fusion.2), kind=kOutput, calls=%fused_computation.64 | convolution fusion | flops 1212874752 | bytes 8271360 | tf_op jit(solution)/shard_map/dot_general | solution.py:164
  224.0 25.8 %all-gather.6.cloned.1.call-done = bf16[1536,512]{1,0:T(8,128)(2,1)} async-done(((bf16[384,512]{1,0:T(8,128)(2,1)}), bf16[1536,512]{1,0:T(8,128)(2,1)}) %all-gather.6.cloned.1.call-update) | async-done | bytes 1572880 | tf_op jit(solution)/shard_map/all_gather | solution.py:8
  252.1 2.0 fusion.39
  (90 shorter events, 16.2 us)
Async XLA Ops:
  6.5 245.6 %copy-start = (bf16[1024,512]{1,0:T(8,128)(2,1)S(1)}, bf16[1024,512]{1,0:T(8,128)(2,1)}, u32[]{:S(2)}) copy-start(bf16[1024,512]{1,0:T(8,128)(2,1)} %param.21) | copy-start | bytes 3145732
  6.5 38.9 %copy-start.1 = (bf16[96,512]{1,0:T(8,128)(2,1)S(1)}, bf16[96,512]{1,0:T(8,128)(2,1)}, u32[]{:S(2)}) copy-start(bf16[96,512]{1,0:T(8,128)(2,1)} %param.11) | copy-start | bytes 294916
  49.4 6.1 %copy-start.5 = (f32[2,16]{1,0:T(2,128)S(1)}, f32[2,16]{1,0:T(2,128)}, u32[]{:S(2)}) copy-start(f32[2,16]{1,0:T(2,128)} %param.18) | copy-start | bytes 388
  50.6 24.0 %all-to-all-start.1 = ((bf16[128,8,512]{2,1,0:T(8,128)(2,1)}), bf16[128,8,512]{2,1,0:T(8,128)(2,1)S(1)}, u32[]{:S(2)}, u32[]{:S(2)}) async-start(bf16[128,8,512]{2,1,0:T(8,128)(2,1)} %bitcast_select_fusion), calls=%async_computation.1 | async-start | bytes 2097152 | tf_op jit(solution)/shard_map/all_to_all | solution.py:133
  74.6 2.4 copy-start.8
  88.5 1.9 copy-start.2
  109.8 3.9 %copy-start.7 = (bf16[2,512,256]{2,1,0:T(8,128)(2,1)S(1)}, bf16[2,512,256]{2,1,0:T(8,128)(2,1)}, u32[]{:S(2)}) copy-start(bf16[2,512,256]{2,1,0:T(8,128)(2,1)} %param.16) | copy-start | bytes 1572868
  109.8 4.5 %copy-start.3 = (bf16[2,512,2048]{2,1,0:T(8,128)(2,1)S(1)}, bf16[2,512,2048]{2,1,0:T(8,128)(2,1)}, u32[]{:S(2)}) copy-start(bf16[2,512,2048]{2,1,0:T(8,128)(2,1)} %param.15) | copy-start | bytes 12582916
  113.4 0.8 copy-start.4
  152.7 24.0 %all-to-all-start.2 = ((bf16[128,8,512]{2,1,0:T(8,128)(2,1)}), bf16[128,8,512]{2,1,0:T(8,128)(2,1)S(1)}, u32[]{:S(2)}, u32[]{:S(2)}) async-start(bf16[128,8,512]{2,1,0:T(8,128)(2,1)} %bitcast.27), calls=%async_computation.2 | async-start | bytes 2097152 | tf_op jit(solution)/shard_map/all_to_all | solution.py:140
  157.4 61.2 %all-gather.4.cloned.1.call-start = ((), (), s32[]{:S(2)}) async-start(), calls=%async_computation.3 | async-start | bytes 3244032 | tf_op jit(solution)/shard_map/all_gather | solution.py:159
  177.7 72.2 %all-gather.6.cloned.1.call-start = ((), (), s32[]{:S(2)}) async-start(), calls=%async_computation.4 | async-start | bytes 1966080 | tf_op jit(solution)/shard_map/all_gather | solution.py:8
  224.0 28.1 %copy-start.6 = (bf16[512,1024]{1,0:T(8,128)(2,1)S(1)}, bf16[512,1024]{1,0:T(8,128)(2,1)}, u32[]{:S(2)}) copy-start(bf16[512,1024]{1,0:T(8,128)(2,1)} %param.20) | copy-start | bytes 3145732
Sparse Core Ops, SparseCore 0:
  177.8 40.6 all-gather.3
  224.2 25.6 all-gather.5
